TPU v7x, 512 devices: a whole 4x8x8 slice. The times are simulated.
512 devices in a mesh: narrow: 4 (over y_hi, core), wide: 128 (over z, x, y_lo).
Axes of the slice: x: 4, y: 8 (y_hi: 2, y_lo: 4; y = y_hi * 4 + y_lo), z: 8, core: 2. Of those that a mesh axis runs over, the one named last changes fastest.
Arguments:
- scan_pair: float32 [2, 4, 2048, 2048], P(None, None, 'wide', 'narrow'), may hold values from -6 to 6
Outputs:
- correlation: float32 [2, 4, 2048, 2048], P(None, None, 'wide', 'narrow')
All inputs are finite; a program needn't handle non-finite values.
Results may differ from a plain program's by a relative error of at most 0.00015.
Values sent between devices are 32-bit elements; how exact they have to be, the bound alone decides.
A program may use at most 64 MiB of HBM per device.

v0:
```python
import math

import jax
import jax.numpy as jnp
from jax import lax
from jax.sharding import PartitionSpec as P

magnitude_floor = 0.25


def partner_2(value, axis, stride):
    mask = 2**stride
    pairs = [(source, source ^ mask) for source in range(lax.axis_size(axis))]
    return lax.ppermute(value, axis, pairs)


def shifted(value, axis, steps):
    count = lax.axis_size(axis)
    pairs = [(source, (source + steps) % count) for source in range(count)]
    return lax.ppermute(value, axis, pairs)


def tables(length, direction):
    indices = jnp.arange(length, dtype=jnp.int32)
    products = indices[:, None] * indices[None, :] % length
    angles = direction * 2.0 * math.pi / length * products.astype(jnp.float32)
    return (jnp.cos(angles), jnp.sin(angles))


def twiddle(radix_one, radix_two, length, direction):
    first_index = jnp.arange(radix_one, dtype=jnp.int32)
    second_index = jnp.arange(radix_two, dtype=jnp.int32)
    products = first_index[:, None] * second_index[None, :] % length
    angles = direction * 2.0 * math.pi / length * products.astype(jnp.float32)
    return (jnp.cos(angles), jnp.sin(angles))


def complex_product(form, left_real, left_imag, right_real, right_imag):

    def single(left, right):
        return jnp.einsum(form, left, right, precision=lax.Precision.HIGHEST)

    real_part = single(left_real, right_real) - single(left_imag, right_imag)
    imag_part = single(left_real, right_imag) + single(left_imag, right_real)
    return (real_part, imag_part)


def forward(real_part, imag_part):
    count, length = real_part.shape
    radix_one = 16
    radix_two = length // radix_one
    real_part = real_part.reshape(count, radix_one, radix_two)
    imag_part = imag_part.reshape(count, radix_one, radix_two)
    small_real, small_imag = tables(radix_one, -1.0)
    real_part, imag_part = complex_product(
        "kz,pzb->pkb", small_real, small_imag, real_part, imag_part
    )
    turn_real, turn_imag = twiddle(radix_one, radix_two, length, -1.0)
    real_part, imag_part = (
        real_part * turn_real - imag_part * turn_imag,
        real_part * turn_imag + imag_part * turn_real,
    )
    large_real, large_imag = tables(radix_two, -1.0)
    real_part, imag_part = complex_product(
        "pkb,bj->pkj", real_part, imag_part, large_real, large_imag
    )
    scale = 1.0 / math.sqrt(length)
    return (real_part * scale, imag_part * scale)


def inverse(real_part, imag_part):
    count, radix_one, radix_two = real_part.shape
    length = radix_one * radix_two
    large_real, large_imag = tables(radix_two, 1.0)
    real_part, imag_part = complex_product(
        "pkj,jb->pkb", real_part, imag_part, large_real, large_imag
    )
    turn_real, turn_imag = twiddle(radix_one, radix_two, length, 1.0)
    real_part, imag_part = (
        real_part * turn_real - imag_part * turn_imag,
        real_part * turn_imag + imag_part * turn_real,
    )
    small_real, small_imag = tables(radix_one, 1.0)
    real_part, imag_part = complex_product(
        "kz,pkb->pzb", small_real, small_imag, real_part, imag_part
    )
    scale = 1.0 / math.sqrt(length)
    return ((real_part * scale).reshape(count, length), (imag_part * scale).reshape(count, length))


def mirror_rows(values):
    for bit_number in range(lax.axis_size("narrow").bit_length() - 1):
        values = partner_2(values, "narrow", bit_number)
    return values


def to_pencils(values):
    received = lax.all_to_all(values, "wide", split_axis=2, concat_axis=1, tiled=True)
    return jnp.transpose(received, (0, 2, 1))


def on_device(scan_pair):
    planes, columns, depth, rows_y = scan_pair.shape
    upper_half = lax.axis_index("narrow") >= lax.axis_size("narrow") // 2
    boundary = shifted(scan_pair[:, :, :, 0:1], "narrow", -1)
    advanced = jnp.concatenate([scan_pair[:, :, :, 1:], boundary], axis=3)

    def arrange(values):
        values = jnp.where(upper_half, jnp.flip(values, (1, 3)), values)
        return jnp.transpose(values, (0, 2, 1, 3)).reshape(planes, depth, columns * rows_y)

    ordered = arrange(scan_pair)
    ordered_next = arrange(advanced)
    partner = mirror_rows(ordered_next)
    both = jnp.concatenate([ordered, partner[0:1], -partner[1:2]], axis=0)
    pencils = to_pencils(both)
    own_rows = pencils[0:2]
    mirrored = pencils[2:4]
    count = own_rows.shape[1]
    spec_real, spec_imag = forward(
        jnp.concatenate([own_rows[0], mirrored[0]], axis=0),
        jnp.concatenate([own_rows[1], mirrored[1]], axis=0),
    )
    own_real = spec_real[:count]
    own_imag = spec_imag[:count]
    twin_real = spec_real[count:]
    twin_imag = spec_imag[count:]
    first_real = (own_real + twin_real) * 0.5
    first_imag = (own_imag + twin_imag) * 0.5
    second_real = (own_imag - twin_imag) * 0.5
    second_imag = -(own_real - twin_real) * 0.5
    cross_real = first_real * second_real + first_imag * second_imag
    cross_imag = first_imag * second_real - first_real * second_imag
    modulus = jnp.maximum(
        jnp.sqrt(cross_real * cross_real + cross_imag * cross_imag), magnitude_floor
    )
    out_real, out_imag = inverse(cross_real / modulus, cross_imag / modulus)
    outgoing = jnp.transpose(jnp.stack([out_real, out_imag]), (0, 2, 1))
    result = lax.all_to_all(outgoing, "wide", split_axis=1, concat_axis=2, tiled=True)
    result = jnp.transpose(result.reshape(planes, depth, columns, rows_y), (0, 2, 1, 3))
    return jnp.where(upper_half, jnp.flip(result, (1, 3)), result)


def solution(mesh):
    return jax.shard_map(
        on_device,
        mesh=mesh,
        in_specs=(P(None, None, "wide", "narrow"),),
        out_specs=P(None, None, "wide", "narrow"),
        check_vma=False,
    )
```

profile of v0, /device:TPU:1, one launch (start us, length us, event | category | flops | bytes accessed | tf_op | source)
XLA Modules:
  0.0 143.9 jit_solution(5781902606828304348)
XLA Ops:
  0.0 0.0 copy-start
  0.0 1.2 copy.33
  1.2 8.7 %collective-permute-start = (f32[2,4,16,1]{3,1,2,0:T(4,128)S(1)}, f32[2,4,16,1]{3,1,2,0:T(4,128)S(1)}, u32[]{:S(2)}, u32[]{:S(2)}) collective-permute-start(f32[2,4,16,1]{3,1,2,0:T(4,128)S(1)} %slice.55), channel_id=1, source_target_pairs={{0,384},{128,0},{256,128},{384,256},{1,385},{129,1},{257,129},{385... | collective-permute-start | bytes 1544 | tf_op jit(solution)/shard_map/ppermute | solution.py:20
  10.0 0.2 slice.54
  10.2 1.9 %collective-permute-done = f32[2,4,16,1]{3,1,2,0:T(4,128)S(1)} collective-permute-done((f32[2,4,16,1]{3,1,2,0:T(4,128)S(1)}, f32[2,4,16,1]{3,1,2,0:T(4,128)S(1)}, u32[]{:S(2)}, u32[]{:S(2)}) %collective-permute-start) | collective-permute-done | bytes 544 | tf_op jit(solution)/shard_map/ppermute | solution.py:20
  12.1 0.1 pad_maximum_fusion.1
  12.2 0.8 rev.11
  13.0 0.1 select_bitcast_fusion
  13.2 0.2 reshape.78
  13.4 1.9 %collective-permute-start.1 = (f32[2,16,2048]{2,1,0:T(8,128)S(1)}, f32[2,16,2048]{2,1,0:T(8,128)S(1)}, u32[]{:S(2)}, u32[]{:S(2)}) collective-permute-start(f32[2,16,2048]{2,1,0:T(8,128)S(1)} %reshape.78), channel_id=1, source_target_pairs={{0,128},{128,0},{256,384},{384,256},{1,129},{129,1},{257,385},{385... | collective-permute-start | bytes 786440 | tf_op jit(solution)/shard_map/ppermute | solution.py:14
  15.3 1.5 %collective-permute-done.1 = f32[2,16,2048]{2,1,0:T(8,128)S(1)} collective-permute-done((f32[2,16,2048]{2,1,0:T(8,128)S(1)}, f32[2,16,2048]{2,1,0:T(8,128)S(1)}, u32[]{:S(2)}, u32[]{:S(2)}) %collective-permute-start.1) | collective-permute-done | bytes 262176 | tf_op jit(solution)/shard_map/ppermute | solution.py:14
  16.8 7.0 %collective-permute-start.2 = (f32[2,16,2048]{2,1,0:T(8,128)S(1)}, f32[2,16,2048]{2,1,0:T(8,128)S(1)}, u32[]{:S(2)}, u32[]{:S(2)}) collective-permute-start(f32[2,16,2048]{2,1,0:T(8,128)S(1)} %collective-permute-done.1), channel_id=1, source_target_pairs={{0,256},{128,384},{256,0},{384,128},{1,257},{129,385},{257,1},{385... | collective-permute-start | bytes 786440 | tf_op jit(solution)/shard_map/ppermute | solution.py:14
  23.8 0.8 rev.10
  24.6 0.0 copy-done
  24.7 0.2 select_bitcast_fusion.1
  24.9 0.2 reshape.77
  25.1 7.1 %collective-permute-done.2 = f32[2,16,2048]{2,1,0:T(8,128)S(1)} collective-permute-done((f32[2,16,2048]{2,1,0:T(8,128)S(1)}, f32[2,16,2048]{2,1,0:T(8,128)S(1)}, u32[]{:S(2)}, u32[]{:S(2)}) %collective-permute-start.2) | collective-permute-done | bytes 262176 | tf_op jit(solution)/shard_map/ppermute | solution.py:14
  32.2 3.1 %copy.37 = f32[4,16,2048]{1,0,2:T(4,128)} copy(f32[4,16,2048]{2,1,0:T(8,128)S(1)} %pad_maximum_fusion) | data formatting | bytes 1048576 | tf_op jit(solution)/shard_map/concatenate | solution.py:115
  35.3 5.4 %reshape.90 = f32[128,1,1024]{2,1,0:T(1,128)} reshape(f32[2048,4,16]{2,1,0:T(4,128)} %bitcast.100) | data formatting | bytes 1048576
  40.7 21.1 %all-to-all-start = ((f32[128,1,1024]{2,1,0:T(1,128)}), f32[128,1,1024]{2,1,0:T(1,128)S(1)}, u32[]{:S(2)}, u32[]{:S(2)}) async-start(f32[128,1,1024]{2,1,0:T(1,128)} %reshape.90), calls=%async_computation | async-start | bytes 1048576 | tf_op jit(solution)/shard_map/all_to_all | solution.py:98
  61.8 0.1 multiply_sine_fusion.8
  61.8 0.1 multiply_sine_fusion.7
  61.9 19.0 %all-to-all-done = f32[128,1,1024]{2,1,0:T(1,128)S(1)} async-done(((f32[128,1,1024]{2,1,0:T(1,128)}), f32[128,1,1024]{2,1,0:T(1,128)S(1)}, u32[]{:S(2)}, u32[]{:S(2)}) %all-to-all-start) | async-done | bytes 524320 | tf_op jit(solution)/shard_map/all_to_all | solution.py:98
  80.9 0.5 broadcast.217
  81.4 1.9 %reduce = f32[128,1024]{1,0:T(8,128)S(1)} reduce(f32[128,1,1024]{2,1,0:T(1,128)S(1)} %all-to-all-done, f32[]{:T(128)} %broadcast.217), dimensions={1}, to_apply=%all_to_all.24.reduce_sub_computation | reduce | bytes 1048580 | tf_op jit(solution)/shard_map/all_to_all | solution.py:98
  83.3 4.3 %reshape.91 = f32[2048,4,16]{2,1,0:T(4,128)} reshape(f32[128,1024]{1,0:T(8,128)S(1)} %reduce) | data formatting | bytes 1048576
  87.6 6.6 %copy.67 = f32[4,16,128,16]{1,2,3,0:T(8,128)} copy(f32[4,16,128,16]{1,0,3,2:T(4,128)} %bitcast.101) | data formatting | bytes 1048576 | tf_op jit(solution)/shard_map/all_to_all | solution.py:98
  94.2 4.9 %all_to_all.27 = f32[4,2048,16]{1,2,0:T(8,128)S(1)} reshape(f32[4,128,16,16]{2,1,3,0:T(8,128)} %bitcast.102) | data formatting | bytes 1048576 | tf_op jit(solution)/shard_map/all_to_all | solution.py:98
  99.2 0.5 fusion.57
  99.8 0.5 fusion.55
  100.3 0.5 fusion.3
  100.8 0.5 fusion.2
  101.2 0.6 fusion.10
  101.9 0.6 fusion.11
  102.5 0.6 fusion
  103.1 0.6 fusion.1
  103.7 0.1 multiply_subtract_fusion.2
  103.8 0.5 fusion.18
  104.3 0.5 fusion.14
  104.9 0.5 convolution_subtract_fusion.3
  105.4 0.5 convolution_add_fusion.3
  106.0 0.3 fusion.27
  106.3 0.3 fusion.28
  106.6 0.3 fusion.5
  107.0 0.3 fusion.7
  107.4 1.0 copy.44
  108.4 1.4 bitcast_bitcast_fusion
  109.8 4.4 %reshape.92 = f32[128,1,512]{2,1,0:T(1,128)S(1)} reshape(f32[2048,2,16]{2,1,0:T(2,128)} %bitcast_bitcast_fusion) | data formatting | bytes 524288
  114.2 18.7 %all_to_all.33 = f32[128,1,512]{2,1,0:T(1,128)S(1)} all-to-all(f32[128,1,512]{2,1,0:T(1,128)S(1)} %reshape.92), channel_id=1, replica_groups=mesh['narrow'=4,'wide'=128] {'wide'}, dimensions={0} | all-to-all | bytes 524288 | tf_op jit(solution)/shard_map/all_to_all | solution.py:139
  132.9 1.3 reduce.1
  134.2 2.8 %reshape.93 = f32[2048,2,16]{2,1,0:T(2,128)S(1)} reshape(f32[128,512]{1,0:T(8,128)S(1)} %reduce.1) | data formatting | bytes 524288
  137.0 2.6 %copy.68 = f32[2,128,16,16]{3,1,2,0:T(8,128)} copy(f32[2,128,16,16]{3,0,2,1:T(2,128)S(1)} %bitcast.103) | data formatting | bytes 524288 | tf_op jit(solution)/shard_map/all_to_all | solution.py:139
  139.5 2.7 %reshape.79 = f32[2,16,4,512]{3,2,1,0:T(4,128)S(1)} reshape(f32[2,16,128,16]{3,2,1,0:T(8,128)} %bitcast.104) | data formatting | bytes 524288 | tf_op jit(solution)/shard_map/reshape | solution.py:140
  142.2 0.8 rev.12
  143.0 0.1 broadcast_select_fusion
  143.1 0.8 copy.47
  (15 shorter events, 0.3 us)
Async XLA Ops:
  0.0 24.6 %copy-start = (f32[2,4,16,512]{3,2,1,0:T(8,128)S(1)}, f32[2,4,16,512]{3,2,1,0:T(8,128)}, u32[]{:S(2)}) copy-start(f32[2,4,16,512]{3,2,1,0:T(8,128)} %param.1) | copy-start | bytes 786436
  1.2 10.9 %collective-permute-start = (f32[2,4,16,1]{3,1,2,0:T(4,128)S(1)}, f32[2,4,16,1]{3,1,2,0:T(4,128)S(1)}, u32[]{:S(2)}, u32[]{:S(2)}) collective-permute-start(f32[2,4,16,1]{3,1,2,0:T(4,128)S(1)} %slice.55), channel_id=1, source_target_pairs={{0,384},{128,0},{256,128},{384,256},{1,385},{129,1},{257,129},{385... | collective-permute-start | bytes 1544 | tf_op jit(solution)/shard_map/ppermute | solution.py:20
  13.4 3.4 %collective-permute-start.1 = (f32[2,16,2048]{2,1,0:T(8,128)S(1)}, f32[2,16,2048]{2,1,0:T(8,128)S(1)}, u32[]{:S(2)}, u32[]{:S(2)}) collective-permute-start(f32[2,16,2048]{2,1,0:T(8,128)S(1)} %reshape.78), channel_id=1, source_target_pairs={{0,128},{128,0},{256,384},{384,256},{1,129},{129,1},{257,385},{385... | collective-permute-start | bytes 786440 | tf_op jit(solution)/shard_map/ppermute | solution.py:14
  16.8 15.3 %collective-permute-start.2 = (f32[2,16,2048]{2,1,0:T(8,128)S(1)}, f32[2,16,2048]{2,1,0:T(8,128)S(1)}, u32[]{:S(2)}, u32[]{:S(2)}) collective-permute-start(f32[2,16,2048]{2,1,0:T(8,128)S(1)} %collective-permute-done.1), channel_id=1, source_target_pairs={{0,256},{128,384},{256,0},{384,128},{1,257},{129,385},{257,1},{385... | collective-permute-start | bytes 786440 | tf_op jit(solution)/shard_map/ppermute | solution.py:14
  40.7 40.2 %all-to-all-start = ((f32[128,1,1024]{2,1,0:T(1,128)}), f32[128,1,1024]{2,1,0:T(1,128)S(1)}, u32[]{:S(2)}, u32[]{:S(2)}) async-start(f32[128,1,1024]{2,1,0:T(1,128)} %reshape.90), calls=%async_computation | async-start | bytes 1048576 | tf_op jit(solution)/shard_map/all_to_all | solution.py:98
where the time goes:
time: 145 us; the launch traced here: 144 us
  local copies, waits for them, and re-layouts  44.9 us (31%)
  starting transfers between devices  38.7 us (27%)
  waiting for transfers between devices  29.5 us (20%)
  blocking collectives  18.7 us (13%)
  matrix products  7.74 us (5%)
  other arithmetic  3.93 us (3%)
    all_to_all x1, starting transfers between devices, to_pencils(): lax.all_to_all(values, 'wide', split_axis=2, concat_axis=1, tiled=True)  21.1 us
    unnamed x15, local copies, waits for them, and re-layouts  19.7 us
    all_to_all x1, waiting for transfers between devices, to_pencils(): lax.all_to_all(values, 'wide', split_axis=2, concat_axis=1, tiled=True)  19 us
    all_to_all x1, blocking collectives, on_device(): lax.all_to_all(outgoing, 'wide', split_axis=1, concat_axis=2, tiled=True)  18.7 us
    all_to_all x3, local copies, waits for them, and re-layouts, to_pencils(): lax.all_to_all(values, 'wide', split_axis=2, concat_axis=1, tiled=True)  12 us
    ppermute x2, starting transfers between devices, partner_2(): return lax.ppermute(value, axis, pairs)  8.93 us
    ppermute x1, starting transfers between devices, shifted(): return lax.ppermute(value, axis, pairs)  8.75 us
    ppermute x2, waiting for transfers between devices, partner_2(): return lax.ppermute(value, axis, pairs)  8.57 us
  transfers between devices with their start and end apart: 4, of which 4 were waited for; matrix products, arithmetic and copies ran while one was open for 1% of the time, Pallas kernels for 0%

commit v1 on v0

v1 whole, which is shorter than its diff:
```python
import functools
import math

import jax
import jax.numpy as jnp
import numpy as np
from jax import lax
from jax.experimental import pallas as pl
from jax.experimental.pallas import tpu as pltpu
from jax.sharding import PartitionSpec as P

magnitude_floor = 0.25
MESH = pl.DeviceIdType.MESH

LINE, PLANE, LANES, ROWS = 16, 32, 128, 512
LENGTH, POINTS = 2048, 16


def constants():
    ka = np.arange(128)
    j = np.arange(128)
    z1 = (j % 8) * 16 + j // 8
    big = np.exp(-2j * np.pi * ((ka[:, None] * z1[None, :]) % 128) / 128)
    forward_big = np.concatenate([big.real, big.imag], axis=0)
    back = np.conj(big).T
    inverse_big = np.concatenate([back.real, back.imag], axis=0)

    z0 = np.arange(POINTS)
    small = np.exp(-2j * np.pi * ((z0[:, None] * z0[None, :]) % POINTS) / POINTS) / math.sqrt(LENGTH)

    def lanes(matrix, columns):
        block = np.einsum("xw,zk->xzwk", columns, matrix).reshape(64, 64)
        return np.block([[block.real, block.imag], [-block.imag, block.real]])

    same, reverse = np.eye(4), np.eye(4)[::-1]
    turn = np.exp(-2j * np.pi * ka[:, None] * z0[None, :] / LENGTH)
    turn = np.tile(turn, (1, 4))
    turn_real = np.concatenate([turn.real, turn.real], axis=1)
    turn_imag = np.concatenate([-turn.imag, turn.imag], axis=1)
    squares = np.stack(
        [
            lanes(small, same),
            lanes(small, reverse),
            lanes(np.conj(small), same),
            turn_real,
            turn_imag,
            np.eye(128)[::-1],
        ]
    )
    return (
        np.stack([forward_big, inverse_big]).astype(np.float32),
        squares.astype(np.float32),
    )


def dot(left, right):
    return jnp.dot(
        left, right, precision=lax.Precision.HIGHEST, preferred_element_type=jnp.float32
    )


def correlate(blocks, first_device, big_ref, square_ref, roll):
    def swap(value):
        return roll(value, 64, 1)

    lane = lax.broadcasted_iota(jnp.int32, (128, LANES), 1)
    real_lane = lane < 64
    sign = jnp.where(real_lane, -1.0, 1.0).astype(jnp.float32)
    turn_real, turn_imag = square_ref[3], square_ref[4]

    both = dot(big_ref[0], jnp.concatenate(blocks, axis=1))
    own, twin = [], []
    for n in range(4):
        upper = both[:128, n * 128 : (n + 1) * 128]
        lower = swap(both[128:, n * 128 : (n + 1) * 128])
        straight = upper + sign * lower
        conjugate = lower - sign * upper
        own.append(straight * turn_real + swap(straight) * turn_imag)
        twin.append(conjugate * turn_real + swap(conjugate) * turn_imag)
    mirrored = [
        jnp.where(first_device, twin[a], twin[b]) for a, b in ((0, 3), (3, 2), (2, 1), (1, 0))
    ]
    spectrum = dot(jnp.concatenate(own, axis=0), square_ref[0])
    mirror_spectrum = dot(jnp.concatenate(mirrored, axis=0), square_ref[1])
    normalized = []
    for n in range(4):
        s = spectrum[n * 128 : (n + 1) * 128]
        m = mirror_spectrum[n * 128 : (n + 1) * 128]
        first = (s + m) * 0.5
        half = (s - m) * 0.5
        turned = first * swap(half)
        plain = first * half
        cross = jnp.where(real_lane, turned - swap(turned), plain + swap(plain))
        square = cross * cross
        modulus = jnp.maximum(jnp.sqrt(square + swap(square)), magnitude_floor)
        normalized.append(cross / modulus)
    back = dot(jnp.concatenate(normalized, axis=0), square_ref[2])
    turned_back = []
    for n in range(4):
        value = back[n * 128 : (n + 1) * 128]
        turned_back.append(value * turn_real - swap(value) * turn_imag)
    both = dot(big_ref[1], jnp.concatenate(turned_back, axis=1))
    return [
        both[:128, n * 128 : (n + 1) * 128] + sign * swap(both[128:, n * 128 : (n + 1) * 128])
        for n in range(4)
    ]


def kernel(
    scan_ref, big_ref, square_ref, out_ref,
    rows, mid, landed, result, mid_back, landed_back,
    send_line, recv_line, send_plane, recv_plane,
    send_plane_back, recv_plane_back, send_line_back, recv_line_back, local,
):
    narrow, wide = lax.axis_index("narrow"), lax.axis_index("wide")
    y_hi, core = narrow // 2, narrow % 2
    z, sheet = wide // 16, wide % 16
    line = core * 8 + z
    plane = y_hi * 16 + sheet
    upper = narrow >= 2
    swap_matrix = square_ref[5]

    def line_peer(step):
        peer = (line + step) % LINE
        return peer, (y_hi * 2 + peer // 8, (peer % 8) * 16 + sheet)

    def plane_peer(step):
        peer = (plane + step) % PLANE
        return peer, ((peer // 16) * 2 + core, z * 16 + peer % 16)

    def exchange(count, peer_of, source, target, mine, send, recv, slot):
        def copy(step):
            peer, device = peer_of(step)
            return pltpu.make_async_remote_copy(
                src_ref=source(peer),
                dst_ref=target(mine),
                send_sem=send.at[step],
                recv_sem=recv.at[step],
                device_id=device,
                device_id_type=MESH,
            )

        def start(step, carry):
            copy(step).start()
            return carry

        def finish(step, carry):
            copy(step).wait()
            return carry

        lax.fori_loop(1, count, start, 0)
        own = pltpu.make_async_copy(source(mine), target(mine), local.at[slot])
        own.start()
        own.wait()
        lax.fori_loop(1, count, finish, 0)

    given = scan_ref[...].reshape(LANES, ROWS)
    parts = [given[:, b * 128 : (b + 1) * 128] for b in range(4)]
    flipped = dot(jnp.concatenate(parts, axis=0), swap_matrix)
    backward = jnp.concatenate(
        [flipped[(3 - b) * 128 : (4 - b) * 128].T for b in range(4)], axis=0
    )
    forward = jnp.concatenate([part.T for part in parts], axis=0)
    ordered = jnp.where(upper, pltpu.roll(backward, 1, 0), forward)
    rows[...] = ordered.reshape(LINE, PLANE, LANES)

    exchange(
        LINE, line_peer, lambda p: rows.at[p], lambda m: mid.at[m], line,
        send_line, recv_line, 0,
    )
    exchange(
        PLANE, plane_peer, lambda p: mid.at[:, p], lambda m: landed.at[m], plane,
        send_plane, recv_plane, 1,
    )

    blocks = [
        landed[16 * (n // 2) : 16 * (n // 2) + 16, 8 * (n % 2) : 8 * (n % 2) + 8, :].reshape(
            128, LANES
        )
        for n in range(4)
    ]
    first_device = line + plane == 0
    outcome = correlate(blocks, first_device, big_ref, square_ref, pltpu.roll)
    for n in range(4):
        result[16 * (n // 2) : 16 * (n // 2) + 16, 8 * (n % 2) : 8 * (n % 2) + 8, :] = outcome[
            n
        ].reshape(16, 8, LANES)

    exchange(
        PLANE, plane_peer, lambda p: result.at[p], lambda m: mid_back.at[m], plane,
        send_plane_back, recv_plane_back, 2,
    )
    exchange(
        LINE, line_peer, lambda p: mid_back.at[:, p], lambda m: landed_back.at[m], line,
        send_line_back, recv_line_back, 3,
    )

    ordered = landed_back[...].reshape(ROWS, LANES)
    turned = dot(
        swap_matrix,
        jnp.concatenate([ordered[b * 128 : (b + 1) * 128] for b in (3, 2, 1, 0)], axis=1),
    )
    backward = jnp.concatenate([turned[:, b * 128 : (b + 1) * 128] for b in range(4)], axis=0)
    ordered = jnp.where(upper, pltpu.roll(backward, 1, 0), ordered)
    final = jnp.concatenate([ordered[b * 128 : (b + 1) * 128].T for b in range(4)], axis=1)
    out_ref[...] = final.reshape(out_ref.shape)


def on_device(scan_pair, big, squares):
    vmem = pl.BlockSpec(memory_space=pltpu.VMEM)
    dma = pltpu.SemaphoreType.DMA
    return pl.pallas_call(
        kernel,
        out_shape=jax.ShapeDtypeStruct(scan_pair.shape, jnp.float32),
        in_specs=[vmem] * 3,
        out_specs=vmem,
        scratch_shapes=[
            pltpu.VMEM((LINE, PLANE, LANES), jnp.float32),
            pltpu.VMEM((LINE, PLANE, LANES), jnp.float32),
            pltpu.VMEM((PLANE, LINE, LANES), jnp.float32),
            pltpu.VMEM((PLANE, LINE, LANES), jnp.float32),
            pltpu.VMEM((PLANE, LINE, LANES), jnp.float32),
            pltpu.VMEM((LINE, PLANE, LANES), jnp.float32),
            dma((LINE,)), dma((LINE,)), dma((PLANE,)), dma((PLANE,)),
            dma((PLANE,)), dma((PLANE,)), dma((LINE,)), dma((LINE,)), dma((4,)),
        ],
        compiler_params=pltpu.CompilerParams(has_side_effects=True),
    )(scan_pair, big, squares)


def solution(mesh):
    big, squares = constants()

    def body(scan_pair):
        return on_device(scan_pair, jnp.asarray(big), jnp.asarray(squares))

    return jax.shard_map(
        body,
        mesh=mesh,
        in_specs=(P(None, None, "wide", "narrow"),),
        out_specs=P(None, None, "wide", "narrow"),
        check_vma=False,
    )
```

time: 145 us -> 67.5 us (0.47)
  Pallas kernels: 0 us -> 64.8 us
  local copies, waits for them, and re-layouts: 44.9 us -> 1.67 us
  starting transfers between devices: 38.7 us -> 0 us
  waiting for transfers between devices: 29.5 us -> 0 us
  blocking collectives: 18.7 us -> 0 us
  matrix products: 7.74 us -> 0 us
  other arithmetic: 3.93 us -> 0 us
    pallas_call x0 -> x1, Pallas kernels: none -> 64.8 us  [on_device(): pl.pallas_call(kernel, out_shape=jax.ShapeDtypeStruct(scan_pair.shape, jn...]
    all_to_all x1 -> x0, starting transfers between devices: 21.1 us -> none  [to_pencils(): lax.all_to_all(values, 'wide', split_axis=2, concat_axis=1, tiled=True)]
    all_to_all x1 -> x0, waiting for transfers between devices: 19 us -> none  [to_pencils(): lax.all_to_all(values, 'wide', split_axis=2, concat_axis=1, tiled=True)]
    all_to_all x1 -> x0, blocking collectives: 18.7 us -> none  [on_device(): lax.all_to_all(outgoing, 'wide', split_axis=1, concat_axis=2, tiled=True)]
    unnamed x15 -> x1, local copies, waits for them, and re-layouts: 19.7 us -> 1.67 us
    ppermute x3 -> x0, starting transfers between devices: 17.7 us -> none  [the longest x2 8.93 us: partner_2(): return lax.ppermute(value, axis, pairs)]
    all_to_all x4 -> x0, local copies, waits for them, and re-layouts: 14.6 us -> none  [the longest x3 12 us: to_pencils(): lax.all_to_all(values, 'wide', split_axis=2, concat_axis=1, tiled=True)]
    ppermute x3 -> x0, waiting for transfers between devices: 10.5 us -> none  [the longest x2 8.57 us: partner_2(): return lax.ppermute(value, axis, pairs)]
  transfers between devices with their start and end apart: 4 -> 0, of which waited for: 4 -> 0; matrix products, arithmetic and copies ran while one was open for 1% -> 0% of each run, Pallas kernels for 0% -> 0%
where the time goes in v1:
time: 67.5 us; the launch traced here: 66.5 us
  Pallas kernels  64.8 us (96%)
  local copies, waits for them, and re-layouts  1.67 us (2%)
    pallas_call x1, Pallas kernels, on_device(): pl.pallas_call(kernel, out_shape=jax.ShapeDtypeStruct(scan_pair.shape, jn...  64.8 us
    unnamed x1, local copies, waits for them, and re-layouts  1.67 us

profile of v1, /device:TPU:1, one launch (start us, length us, event | category | flops | bytes accessed | tf_op | source)
XLA Modules:
  0.0 66.5 jit_solution(9785113263922783588)
XLA Ops:
  0.0 64.8 %shard_map.37 = f32[2,4,16,512]{3,2,1,0:T(8,128)} custom-call(f32[2,4,16,512]{3,2,1,0:T(8,128)} %scan_ref.1, f32[2,256,128]{2,1,0:T(8,128)} %constant.4.clone.big_ref, f32[6,128,128]{2,1,0:T(8,128)} %constant.5.clone.square_ref), custom_call_target="tpu_custom_call" | custom-call | tf_op jit(solution)/shard_map/pallas_call | solution.py:212
  64.9 1.7 %copy.5 = f32[2,4,16,512]{3,2,1,0:T(8,128)} copy(f32[2,4,16,512]{3,2,1,0:T(8,128)} %shard_map.37) | data formatting | bytes 524288

commit v2 on v1

--- a/solution.py
+++ b/solution.py
@@ -154,6 +154,20 @@
         own.wait()
         lax.fori_loop(1, count, finish, 0)
 
+    barrier = pltpu.get_barrier_semaphore()
+
+    def greet(peer_of):
+        def signal(step, carry):
+            pl.semaphore_signal(
+                barrier, inc=1, device_id=peer_of(step)[1], device_id_type=MESH
+            )
+            return carry
+
+        return signal
+
+    lax.fori_loop(1, PLANE, greet(plane_peer), 0)
+    lax.fori_loop(1, LINE, greet(line_peer), 0)
+
     given = scan_ref[...].reshape(LANES, ROWS)
     parts = [given[:, b * 128 : (b + 1) * 128] for b in range(4)]
     flipped = dot(jnp.concatenate(parts, axis=0), swap_matrix)
@@ -163,6 +177,7 @@
     forward = jnp.concatenate([part.T for part in parts], axis=0)
     ordered = jnp.where(upper, pltpu.roll(backward, 1, 0), forward)
     rows[...] = ordered.reshape(LINE, PLANE, LANES)
+    pl.semaphore_wait(barrier, LINE + PLANE - 2)
 
     exchange(
         LINE, line_peer, lambda p: rows.at[p], lambda m: mid.at[m], line,
@@ -224,7 +239,7 @@
             dma((LINE,)), dma((LINE,)), dma((PLANE,)), dma((PLANE,)),
             dma((PLANE,)), dma((PLANE,)), dma((LINE,)), dma((LINE,)), dma((4,)),
         ],
-        compiler_params=pltpu.CompilerParams(has_side_effects=True),
+        compiler_params=pltpu.CompilerParams(collective_id=0, has_side_effects=True),
     )(scan_pair, big, squares)
 
 

time: 67.5 us -> 58.1 us (0.86); the launches traced: 66.5 us -> 57.9 us
  Pallas kernels: 64.8 us -> 56.2 us
    pallas_call x1, Pallas kernels: 64.8 us -> 56.2 us  [on_device(): pl.pallas_call(kernel, out_shape=jax.ShapeDtypeStruct(scan_pair.shape, jn...]
where the time goes in v2:
time: 58.1 us; the launch traced here: 57.9 us
  Pallas kernels  56.2 us (97%)
  local copies, waits for them, and re-layouts  1.67 us (3%)
    pallas_call x1, Pallas kernels, on_device(): pl.pallas_call(kernel, out_shape=jax.ShapeDtypeStruct(scan_pair.shape, jn...  56.2 us
    unnamed x1, local copies, waits for them, and re-layouts  1.67 us

profile of v2, /device:TPU:1, one launch (start us, length us, event | category | flops | bytes accessed | tf_op | source)
XLA Modules:
  0.0 57.9 jit_solution(7336151573065661006)
XLA Ops:
  0.0 56.2 %shard_map.37 = f32[2,4,16,512]{3,2,1,0:T(8,128)} custom-call(f32[2,4,16,512]{3,2,1,0:T(8,128)} %scan_ref.1, f32[2,256,128]{2,1,0:T(8,128)} %constant.4.clone.big_ref, f32[6,128,128]{2,1,0:T(8,128)} %constant.5.clone.square_ref), custom_call_target="tpu_custom_call" | custom-call | tf_op jit(solution)/shard_map/pallas_call | solution.py:227
  56.2 1.7 %copy.5 = f32[2,4,16,512]{3,2,1,0:T(8,128)} copy(f32[2,4,16,512]{3,2,1,0:T(8,128)} %shard_map.37) | data formatting | bytes 524288

commit v3 on v2

--- a/solution.py
+++ b/solution.py
@@ -108,9 +108,9 @@
 
 def kernel(
     scan_ref, big_ref, square_ref, out_ref,
-    rows, mid, landed, result, mid_back, landed_back,
+    rows, mid, landed, result, paired, arrived,
     send_line, recv_line, send_plane, recv_plane,
-    send_plane_back, recv_plane_back, send_line_back, recv_line_back, local,
+    send_core, recv_core, send_back, recv_back, local,
 ):
     narrow, wide = lax.axis_index("narrow"), lax.axis_index("wide")
     y_hi, core = narrow // 2, narrow % 2
@@ -170,13 +170,20 @@
 
     given = scan_ref[...].reshape(LANES, ROWS)
     parts = [given[:, b * 128 : (b + 1) * 128] for b in range(4)]
-    flipped = dot(jnp.concatenate(parts, axis=0), swap_matrix)
-    backward = jnp.concatenate(
-        [flipped[(3 - b) * 128 : (4 - b) * 128].T for b in range(4)], axis=0
-    )
-    forward = jnp.concatenate([part.T for part in parts], axis=0)
-    ordered = jnp.where(upper, pltpu.roll(backward, 1, 0), forward)
-    rows[...] = ordered.reshape(LINE, PLANE, LANES)
+
+    @pl.when(upper)
+    def _():
+        flipped = dot(jnp.concatenate(parts, axis=0), swap_matrix)
+        backward = jnp.concatenate(
+            [flipped[(3 - b) * 128 : (4 - b) * 128].T for b in range(4)], axis=0
+        )
+        rows[...] = pltpu.roll(backward, 1, 0).reshape(LINE, PLANE, LANES)
+
+    @pl.when(jnp.logical_not(upper))
+    def _():
+        forward = jnp.concatenate([part.T for part in parts], axis=0)
+        rows[...] = forward.reshape(LINE, PLANE, LANES)
+
     pl.semaphore_wait(barrier, LINE + PLANE - 2)
 
     exchange(
@@ -197,50 +204,114 @@
     first_device = line + plane == 0
     outcome = correlate(blocks, first_device, big_ref, square_ref, pltpu.roll)
     for n in range(4):
-        result[16 * (n // 2) : 16 * (n // 2) + 16, 8 * (n % 2) : 8 * (n % 2) + 8, :] = outcome[
-            n
-        ].reshape(16, 8, LANES)
-
-    exchange(
-        PLANE, plane_peer, lambda p: result.at[p], lambda m: mid_back.at[m], plane,
-        send_plane_back, recv_plane_back, 2,
-    )
-    exchange(
-        LINE, line_peer, lambda p: mid_back.at[:, p], lambda m: landed_back.at[m], line,
-        send_line_back, recv_line_back, 3,
-    )
-
-    ordered = landed_back[...].reshape(ROWS, LANES)
-    turned = dot(
-        swap_matrix,
-        jnp.concatenate([ordered[b * 128 : (b + 1) * 128] for b in (3, 2, 1, 0)], axis=1),
-    )
-    backward = jnp.concatenate([turned[:, b * 128 : (b + 1) * 128] for b in range(4)], axis=0)
-    ordered = jnp.where(upper, pltpu.roll(backward, 1, 0), ordered)
-    final = jnp.concatenate([ordered[b * 128 : (b + 1) * 128].T for b in range(4)], axis=1)
+        result[n % 2, (n // 2) * 128 : (n // 2) * 128 + 128, :] = outcome[n]
+
+    place = z * 32 + plane
+    place_mirror = (256 - place) % 256
+    other = 1 - core
+    slots = (core, jnp.where(place == 0, core, other))
+    partner = (y_hi * 2 + other, wide)
+
+    def half(half_index):
+        return pl.ds(half_index * 128, 128)
+
+    swaps = [
+        pltpu.make_async_remote_copy(
+            src_ref=result.at[other, half(h)],
+            dst_ref=paired.at[slots[h], half(h)],
+            send_sem=send_core.at[h],
+            recv_sem=recv_core.at[h],
+            device_id=partner,
+            device_id_type=MESH,
+        )
+        for h in range(2)
+    ]
+    keeps = [
+        pltpu.make_async_copy(
+            result.at[core, half(h)], paired.at[slots[h], half(h)], local.at[2 + h]
+        )
+        for h in range(2)
+    ]
+    for copy in swaps + keeps:
+        copy.start()
+    for copy in swaps + keeps:
+        copy.wait()
+
+    x, y = sheet // 4, y_hi * 4 + sheet % 4
+    for far_x in (2, 1, 3, 0):
+        to_x = (x + far_x) % 4
+
+        def row_of_chips(step, carry, to_x=to_x, far_x=far_x):
+            bend = (step + 1) // 2
+            to_y = (y + 4 + jnp.where(step % 2 == 1, -bend, bend)) % 8
+            to_half, to_sheet = to_y // 4, to_x * 4 + to_y % 4
+            to_place = jnp.where(to_half == 0, place, place_mirror)
+            for far_z in (4, 3, 5, 2, 6, 1, 7, 0):
+                to_z = (z + far_z) % 8
+                copy = pltpu.make_async_remote_copy(
+                    src_ref=paired.at[:, (to_half * 16 + to_sheet) * 8 + to_z],
+                    dst_ref=arrived.at[:, to_place],
+                    send_sem=send_back.at[0],
+                    recv_sem=recv_back.at[0],
+                    device_id=(to_half * 2 + core, to_z * 16 + to_sheet),
+                    device_id_type=MESH,
+                )
+                if far_x == 0 and far_z == 0:
+                    pl.when(step < 7)(copy.start)
+                else:
+                    copy.start()
+            return carry
+
+        lax.fori_loop(0, 8, row_of_chips, 0)
+    own = pltpu.make_async_copy(
+        paired.at[:, plane_row(y_hi, sheet, z)],
+        arrived.at[:, jnp.where(y_hi == 0, place, place_mirror)],
+        local.at[4],
+    )
+    own.start()
+    own.wait()
+    everything = arrived.at[:, pl.ds(0, 255)]
+    pltpu.make_async_copy(everything, everything, send_back.at[0]).wait()
+    pltpu.make_async_copy(everything, everything, recv_back.at[0]).wait()
+    out_ref[...] = arrived[...].reshape(ROWS, LANES)
+
+
+def plane_row(y_hi, sheet, z):
+    return (y_hi * 16 + sheet) * 8 + z
+
+
+def turn_kernel(rows_ref, out_ref):
+    rows = rows_ref[...]
+    final = jnp.concatenate([rows[b * 128 : (b + 1) * 128].T for b in range(4)], axis=1)
     out_ref[...] = final.reshape(out_ref.shape)
 
 
 def on_device(scan_pair, big, squares):
     vmem = pl.BlockSpec(memory_space=pltpu.VMEM)
     dma = pltpu.SemaphoreType.DMA
-    return pl.pallas_call(
+    exchanged = pl.pallas_call(
         kernel,
-        out_shape=jax.ShapeDtypeStruct(scan_pair.shape, jnp.float32),
+        out_shape=jax.ShapeDtypeStruct((ROWS, LANES), jnp.float32),
         in_specs=[vmem] * 3,
         out_specs=vmem,
         scratch_shapes=[
             pltpu.VMEM((LINE, PLANE, LANES), jnp.float32),
             pltpu.VMEM((LINE, PLANE, LANES), jnp.float32),
             pltpu.VMEM((PLANE, LINE, LANES), jnp.float32),
-            pltpu.VMEM((PLANE, LINE, LANES), jnp.float32),
-            pltpu.VMEM((PLANE, LINE, LANES), jnp.float32),
-            pltpu.VMEM((LINE, PLANE, LANES), jnp.float32),
+            pltpu.VMEM((2, 256, LANES), jnp.float32),
+            pltpu.VMEM((2, 256, LANES), jnp.float32),
+            pltpu.VMEM((2, 256, LANES), jnp.float32),
             dma((LINE,)), dma((LINE,)), dma((PLANE,)), dma((PLANE,)),
-            dma((PLANE,)), dma((PLANE,)), dma((LINE,)), dma((LINE,)), dma((4,)),
+            dma((2,)), dma((2,)), dma((1,)), dma((1,)), dma((5,)),
         ],
         compiler_params=pltpu.CompilerParams(collective_id=0, has_side_effects=True),
     )(scan_pair, big, squares)
+    return pl.pallas_call(
+        turn_kernel,
+        out_shape=jax.ShapeDtypeStruct(scan_pair.shape, jnp.float32),
+        in_specs=[vmem],
+        out_specs=vmem,
+    )(exchanged)
 
 
 def solution(mesh):

time: 58.1 us -> 52.5 us (0.904)
  Pallas kernels: 56.2 us -> 52.3 us
  local copies, waits for them, and re-layouts: 1.67 us -> 0 us
    pallas_call x1 -> x2, Pallas kernels: 56.2 us -> 52.3 us  [the longest x1 50.5 us: on_device(): pl.pallas_call(kernel, out_shape=jax.ShapeDtypeStruct((ROWS, LANES), jnp....]
    unnamed x1 -> x0, local copies, waits for them, and re-layouts: 1.67 us -> none
where the time goes in v3:
time: 52.5 us; the launch traced here: 52.3 us
  Pallas kernels  52.3 us (100%)
    pallas_call x1, Pallas kernels, on_device(): pl.pallas_call(kernel, out_shape=jax.ShapeDtypeStruct((ROWS, LANES), jnp....  50.5 us
    pallas_call x1, Pallas kernels, on_device(): pl.pallas_call(turn_kernel, out_shape=jax.ShapeDtypeStruct(scan_pair.shap...  1.79 us

profile of v3, /device:TPU:1, one launch (start us, length us, event | category | flops | bytes accessed | tf_op | source)
XLA Modules:
  0.0 52.3 jit_solution(17479083246040970495)
XLA Ops:
  0.0 50.5 %shard_map.37.rows_ref = f32[512,128]{1,0:T(8,128)} custom-call(f32[2,4,16,512]{3,2,1,0:T(8,128)} %scan_ref.1, f32[2,256,128]{2,1,0:T(8,128)} %constant.4.clone.big_ref, f32[6,128,128]{2,1,0:T(8,128)} %constant.5.clone.square_ref), custom_call_target="tpu_custom_call" | custom-call | tf_op jit(solution)/shard_map/pallas_call | solution.py:292
  50.5 1.8 %shard_map.38 = f32[2,4,16,512]{3,2,1,0:T(8,128)} custom-call(f32[512,128]{1,0:T(8,128)} %shard_map.37.rows_ref), custom_call_target="tpu_custom_call" | custom-call | tf_op jit(solution)/shard_map/pallas_call | solution.py:309

commit v4 on v3

--- a/solution.py
+++ b/solution.py
@@ -116,7 +116,8 @@
     y_hi, core = narrow // 2, narrow % 2
     z, sheet = wide // 16, wide % 16
     line = core * 8 + z
-    plane = y_hi * 16 + sheet
+    x, y = sheet // 4, y_hi * 4 + sheet % 4
+    plane = x * 8 + y
     upper = narrow >= 2
     swap_matrix = square_ref[5]
 
@@ -125,34 +126,38 @@
         return peer, (y_hi * 2 + peer // 8, (peer % 8) * 16 + sheet)
 
     def plane_peer(step):
-        peer = (plane + step) % PLANE
-        return peer, ((peer // 16) * 2 + core, z * 16 + peer % 16)
-
-    def exchange(count, peer_of, source, target, mine, send, recv, slot):
-        def copy(step):
-            peer, device = peer_of(step)
-            return pltpu.make_async_remote_copy(
-                src_ref=source(peer),
-                dst_ref=target(mine),
-                send_sem=send.at[step],
-                recv_sem=recv.at[step],
-                device_id=device,
-                device_id_type=MESH,
-            )
-
-        def start(step, carry):
-            copy(step).start()
+        to_x, to_y = (x + step // 8) % 4, (y + step) % 8
+        return to_x * 8 + to_y, ((to_y // 4) * 2 + core, z * 16 + to_x * 4 + to_y % 4)
+
+    def line_copy(far_x, step):
+        peer, device = line_peer(step)
+        first = pl.multiple_of(((x + far_x) % 4) * 8, 8)
+        return pltpu.make_async_remote_copy(
+            src_ref=rows.at[peer, pl.ds(first, 8)],
+            dst_ref=mid.at[line, pl.ds(first, 8)],
+            send_sem=send_line.at[far_x, step],
+            recv_sem=recv_line.at[far_x, step],
+            device_id=device,
+            device_id_type=MESH,
+        )
+
+    def plane_copy(step):
+        peer, device = plane_peer(step)
+        return pltpu.make_async_remote_copy(
+            src_ref=mid.at[:, peer],
+            dst_ref=landed.at[x, y],
+            send_sem=send_plane.at[step],
+            recv_sem=recv_plane.at[step],
+            device_id=device,
+            device_id_type=MESH,
+        )
+
+    def each(low, high, act):
+        def body(step, carry):
+            act(step)
             return carry
 
-        def finish(step, carry):
-            copy(step).wait()
-            return carry
-
-        lax.fori_loop(1, count, start, 0)
-        own = pltpu.make_async_copy(source(mine), target(mine), local.at[slot])
-        own.start()
-        own.wait()
-        lax.fori_loop(1, count, finish, 0)
+        lax.fori_loop(low, high, body, 0)
 
     barrier = pltpu.get_barrier_semaphore()
 
@@ -186,19 +191,26 @@
 
     pl.semaphore_wait(barrier, LINE + PLANE - 2)
 
-    exchange(
-        LINE, line_peer, lambda p: rows.at[p], lambda m: mid.at[m], line,
-        send_line, recv_line, 0,
-    )
-    exchange(
-        PLANE, plane_peer, lambda p: mid.at[:, p], lambda m: landed.at[m], plane,
-        send_plane, recv_plane, 1,
-    )
+    parts_order = (2, 1, 3, 0)
+    for far_x in parts_order:
+        each(1, LINE, lambda step: line_copy(far_x, step).start())
+    own = pltpu.make_async_copy(rows.at[line], mid.at[line], local.at[0])
+    own.start()
+    own.wait()
+    for far_x in parts_order:
+        each(1, LINE, lambda step: line_copy(far_x, step).wait_recv())
+        each(max(far_x * 8, 1), far_x * 8 + 8, lambda step: plane_copy(step).start())
+    own = pltpu.make_async_copy(mid.at[:, plane], landed.at[x, y], local.at[1])
+    own.start()
+    own.wait()
+    for far_x in parts_order:
+        each(1, LINE, lambda step: line_copy(far_x, step).wait_send())
+    each(1, PLANE, lambda step: plane_copy(step).wait())
 
     blocks = [
-        landed[16 * (n // 2) : 16 * (n // 2) + 16, 8 * (n % 2) : 8 * (n % 2) + 8, :].reshape(
-            128, LANES
-        )
+        landed[
+            :, 4 * (n // 2) : 4 * (n // 2) + 4, 8 * (n % 2) : 8 * (n % 2) + 8, :
+        ].reshape(128, LANES)
         for n in range(4)
     ]
     first_device = line + plane == 0
@@ -237,7 +249,6 @@
     for copy in swaps + keeps:
         copy.wait()
 
-    x, y = sheet // 4, y_hi * 4 + sheet % 4
     for far_x in (2, 1, 3, 0):
         to_x = (x + far_x) % 4
 
@@ -297,11 +308,11 @@
         scratch_shapes=[
             pltpu.VMEM((LINE, PLANE, LANES), jnp.float32),
             pltpu.VMEM((LINE, PLANE, LANES), jnp.float32),
-            pltpu.VMEM((PLANE, LINE, LANES), jnp.float32),
+            pltpu.VMEM((4, 8, LINE, LANES), jnp.float32),
             pltpu.VMEM((2, 256, LANES), jnp.float32),
             pltpu.VMEM((2, 256, LANES), jnp.float32),
             pltpu.VMEM((2, 256, LANES), jnp.float32),
-            dma((LINE,)), dma((LINE,)), dma((PLANE,)), dma((PLANE,)),
+            dma((4, LINE)), dma((4, LINE)), dma((PLANE,)), dma((PLANE,)),
             dma((2,)), dma((2,)), dma((1,)), dma((1,)), dma((5,)),
         ],
         compiler_params=pltpu.CompilerParams(collective_id=0, has_side_effects=True),

time: 52.5 us -> 51.6 us (0.983)
  Pallas kernels: 52.3 us -> 51.5 us
    pallas_call x1, Pallas kernels: 50.5 us -> 49.7 us  [on_device(): pl.pallas_call(kernel, out_shape=jax.ShapeDtypeStruct((ROWS, LANES), jnp....]
where the time goes in v4:
time: 51.6 us; the launch traced here: 51.5 us
  Pallas kernels  51.5 us (100%)
    pallas_call x1, Pallas kernels, on_device(): pl.pallas_call(kernel, out_shape=jax.ShapeDtypeStruct((ROWS, LANES), jnp....  49.7 us
    pallas_call x1, Pallas kernels, on_device(): pl.pallas_call(turn_kernel, out_shape=jax.ShapeDtypeStruct(scan_pair.shap...  1.79 us

profile of v4, /device:TPU:1, one launch (start us, length us, event | category | flops | bytes accessed | tf_op | source)
XLA Modules:
  0.0 51.5 jit_solution(13742103752243499995)
XLA Ops:
  0.0 49.7 %shard_map.37.rows_ref = f32[512,128]{1,0:T(8,128)} custom-call(f32[2,4,16,512]{3,2,1,0:T(8,128)} %scan_ref.1, f32[2,256,128]{2,1,0:T(8,128)} %constant.4.clone.big_ref, f32[6,128,128]{2,1,0:T(8,128)} %constant.5.clone.square_ref), custom_call_target="tpu_custom_call" | custom-call | tf_op jit(solution)/shard_map/pallas_call | solution.py:303
  49.7 1.8 %shard_map.38 = f32[2,4,16,512]{3,2,1,0:T(8,128)} custom-call(f32[512,128]{1,0:T(8,128)} %shard_map.37.rows_ref), custom_call_target="tpu_custom_call" | custom-call | tf_op jit(solution)/shard_map/pallas_call | solution.py:320

commit v5 on v4

--- a/solution.py
+++ b/solution.py
@@ -3,6 +3,7 @@
 
 import jax
 import jax.numpy as jnp
+import ml_dtypes
 import numpy as np
 from jax import lax
 from jax.experimental import pallas as pl
@@ -37,20 +38,28 @@
     turn = np.tile(turn, (1, 4))
     turn_real = np.concatenate([turn.real, turn.real], axis=1)
     turn_imag = np.concatenate([-turn.imag, turn.imag], axis=1)
-    squares = np.stack(
-        [
-            lanes(small, same),
-            lanes(small, reverse),
-            lanes(np.conj(small), same),
-            turn_real,
-            turn_imag,
-            np.eye(128)[::-1],
-        ]
+    factors = [lanes(small, same), lanes(small, reverse), lanes(np.conj(small), same)]
+    turns = np.stack([turn_real, turn_imag, np.eye(128)[::-1]]).astype(np.float32)
+    return (
+        np.stack([left_factor(forward_big), left_factor(inverse_big)]),
+        np.stack([right_factor(factor) for factor in factors]),
+        turns,
     )
-    return (
-        np.stack([forward_big, inverse_big]).astype(np.float32),
-        squares.astype(np.float32),
-    )
+
+
+def pieces(matrix):
+    high = matrix.astype(ml_dtypes.bfloat16)
+    return high, (matrix - high.astype(np.float64)).astype(ml_dtypes.bfloat16)
+
+
+def left_factor(matrix):
+    high, low = pieces(matrix)
+    return np.block([[high, high], [low, np.zeros_like(low)]])
+
+
+def right_factor(matrix):
+    high, low = pieces(matrix)
+    return np.block([[high, low], [high, np.zeros_like(low)]])
 
 
 def dot(left, right):
@@ -59,16 +68,32 @@
     )
 
 
-def correlate(blocks, first_device, big_ref, square_ref, roll):
+def split(value, axis):
+    high = value.astype(jnp.bfloat16)
+    low = (value - high.astype(jnp.float32)).astype(jnp.bfloat16)
+    return jnp.concatenate([high, low], axis=axis)
+
+
+def times_left(factor, value):
+    product = jnp.dot(factor, split(value, 0), preferred_element_type=jnp.float32)
+    return product[:256] + product[256:]
+
+
+def times_right(value, factor):
+    product = jnp.dot(split(value, 1), factor, preferred_element_type=jnp.float32)
+    return product[:, :128] + product[:, 128:]
+
+
+def correlate(blocks, first_device, big_ref, small_ref, turn_ref, roll):
     def swap(value):
         return roll(value, 64, 1)
 
     lane = lax.broadcasted_iota(jnp.int32, (128, LANES), 1)
     real_lane = lane < 64
     sign = jnp.where(real_lane, -1.0, 1.0).astype(jnp.float32)
-    turn_real, turn_imag = square_ref[3], square_ref[4]
-
-    both = dot(big_ref[0], jnp.concatenate(blocks, axis=1))
+    turn_real, turn_imag = turn_ref[0], turn_ref[1]
+
+    both = times_left(big_ref[0], jnp.concatenate(blocks, axis=1))
     own, twin = [], []
     for n in range(4):
         upper = both[:128, n * 128 : (n + 1) * 128]
@@ -80,8 +105,8 @@
     mirrored = [
         jnp.where(first_device, twin[a], twin[b]) for a, b in ((0, 3), (3, 2), (2, 1), (1, 0))
     ]
-    spectrum = dot(jnp.concatenate(own, axis=0), square_ref[0])
-    mirror_spectrum = dot(jnp.concatenate(mirrored, axis=0), square_ref[1])
+    spectrum = times_right(jnp.concatenate(own, axis=0), small_ref[0])
+    mirror_spectrum = times_right(jnp.concatenate(mirrored, axis=0), small_ref[1])
     normalized = []
     for n in range(4):
         s = spectrum[n * 128 : (n + 1) * 128]
@@ -94,12 +119,12 @@
         square = cross * cross
         modulus = jnp.maximum(jnp.sqrt(square + swap(square)), magnitude_floor)
         normalized.append(cross / modulus)
-    back = dot(jnp.concatenate(normalized, axis=0), square_ref[2])
+    back = times_right(jnp.concatenate(normalized, axis=0), small_ref[2])
     turned_back = []
     for n in range(4):
         value = back[n * 128 : (n + 1) * 128]
         turned_back.append(value * turn_real - swap(value) * turn_imag)
-    both = dot(big_ref[1], jnp.concatenate(turned_back, axis=1))
+    both = times_left(big_ref[1], jnp.concatenate(turned_back, axis=1))
     return [
         both[:128, n * 128 : (n + 1) * 128] + sign * swap(both[128:, n * 128 : (n + 1) * 128])
         for n in range(4)
@@ -107,10 +132,10 @@
 
 
 def kernel(
-    scan_ref, big_ref, square_ref, out_ref,
-    rows, mid, landed, result, paired, arrived,
+    scan_hbm, big_hbm, small_hbm, turn_hbm, out_ref,
+    scan_ref, big_ref, small_ref, turn_ref, rows, mid, landed, result, paired, arrived,
     send_line, recv_line, send_plane, recv_plane,
-    send_core, recv_core, send_back, recv_back, local,
+    send_core, recv_core, send_back, recv_back, local, load,
 ):
     narrow, wide = lax.axis_index("narrow"), lax.axis_index("wide")
     y_hi, core = narrow // 2, narrow % 2
@@ -119,7 +144,19 @@
     x, y = sheet // 4, y_hi * 4 + sheet % 4
     plane = x * 8 + y
     upper = narrow >= 2
-    swap_matrix = square_ref[5]
+    loads = [
+        pltpu.make_async_copy(source, target, load.at[i])
+        for i, (source, target) in enumerate(
+            [
+                (scan_hbm, scan_ref),
+                (turn_hbm, turn_ref),
+                (big_hbm, big_ref),
+                (small_hbm, small_ref),
+            ]
+        )
+    ]
+    for copy in loads:
+        copy.start()
 
     def line_peer(step):
         peer = (line + step) % LINE
@@ -173,6 +210,9 @@
     lax.fori_loop(1, PLANE, greet(plane_peer), 0)
     lax.fori_loop(1, LINE, greet(line_peer), 0)
 
+    loads[0].wait()
+    loads[1].wait()
+    swap_matrix = turn_ref[2]
     given = scan_ref[...].reshape(LANES, ROWS)
     parts = [given[:, b * 128 : (b + 1) * 128] for b in range(4)]
 
@@ -213,8 +253,10 @@
         ].reshape(128, LANES)
         for n in range(4)
     ]
+    loads[2].wait()
+    loads[3].wait()
     first_device = line + plane == 0
-    outcome = correlate(blocks, first_device, big_ref, square_ref, pltpu.roll)
+    outcome = correlate(blocks, first_device, big_ref, small_ref, turn_ref, pltpu.roll)
     for n in range(4):
         result[n % 2, (n // 2) * 128 : (n // 2) * 128 + 128, :] = outcome[n]
 
@@ -297,15 +339,19 @@
     out_ref[...] = final.reshape(out_ref.shape)
 
 
-def on_device(scan_pair, big, squares):
+def on_device(scan_pair, big, small, turns):
     vmem = pl.BlockSpec(memory_space=pltpu.VMEM)
     dma = pltpu.SemaphoreType.DMA
     exchanged = pl.pallas_call(
         kernel,
         out_shape=jax.ShapeDtypeStruct((ROWS, LANES), jnp.float32),
-        in_specs=[vmem] * 3,
+        in_specs=[pl.BlockSpec(memory_space=pl.ANY)] * 4,
         out_specs=vmem,
         scratch_shapes=[
+            pltpu.VMEM(scan_pair.shape, jnp.float32),
+            pltpu.VMEM(big.shape, jnp.bfloat16),
+            pltpu.VMEM(small.shape, jnp.bfloat16),
+            pltpu.VMEM(turns.shape, jnp.float32),
             pltpu.VMEM((LINE, PLANE, LANES), jnp.float32),
             pltpu.VMEM((LINE, PLANE, LANES), jnp.float32),
             pltpu.VMEM((4, 8, LINE, LANES), jnp.float32),
@@ -313,10 +359,10 @@
             pltpu.VMEM((2, 256, LANES), jnp.float32),
             pltpu.VMEM((2, 256, LANES), jnp.float32),
             dma((4, LINE)), dma((4, LINE)), dma((PLANE,)), dma((PLANE,)),
-            dma((2,)), dma((2,)), dma((1,)), dma((1,)), dma((5,)),
+            dma((2,)), dma((2,)), dma((1,)), dma((1,)), dma((5,)), dma((4,)),
         ],
         compiler_params=pltpu.CompilerParams(collective_id=0, has_side_effects=True),
-    )(scan_pair, big, squares)
+    )(scan_pair, big, small, turns)
     return pl.pallas_call(
         turn_kernel,
         out_shape=jax.ShapeDtypeStruct(scan_pair.shape, jnp.float32),
@@ -326,10 +372,10 @@
 
 
 def solution(mesh):
-    big, squares = constants()
+    tables = constants()
 
     def body(scan_pair):
-        return on_device(scan_pair, jnp.asarray(big), jnp.asarray(squares))
+        return on_device(scan_pair, *(jnp.asarray(table) for table in tables))
 
     return jax.shard_map(
         body,

time: 51.6 us -> 49.4 us (0.957)
  Pallas kernels: 51.5 us -> 49.3 us
    pallas_call x1, Pallas kernels: 49.7 us -> 47.5 us  [on_device(): pl.pallas_call(kernel, out_shape=jax.ShapeDtypeStruct((ROWS, LANES), jnp....]
where the time goes in v5:
time: 49.4 us; the launch traced here: 49.3 us
  Pallas kernels  49.3 us (100%)
    pallas_call x1, Pallas kernels, on_device(): pl.pallas_call(kernel, out_shape=jax.ShapeDtypeStruct((ROWS, LANES), jnp....  47.5 us
    pallas_call x1, Pallas kernels, on_device(): pl.pallas_call(turn_kernel, out_shape=jax.ShapeDtypeStruct(scan_pair.shap...  1.79 us

profile of v5, /device:TPU:1, one launch (start us, length us, event | category | flops | bytes accessed | tf_op | source)
XLA Modules:
  0.0 49.3 jit_solution(107957962896577992)
XLA Ops:
  0.0 47.5 %shard_map.46.rows_ref = f32[512,128]{1,0:T(8,128)} custom-call(f32[2,4,16,512]{3,2,1,0:T(8,128)} %scan_hbm.1, bf16[2,512,256]{2,1,0:T(8,128)(2,1)} %constant.6.clone.big_hbm, bf16[3,256,256]{2,1,0:T(8,128)(2,1)} %constant.7.clone.small_hbm, f32[3,128,128]{2,1,0:T(8,128)} %constant.8.clone.turn_hbm), custom_call_target="tpu_custom_call" | custom-call | tf_op jit(solution)/shard_map/pallas_call | solution.py:345
  47.5 1.8 %shard_map.47 = f32[2,4,16,512]{3,2,1,0:T(8,128)} custom-call(f32[512,128]{1,0:T(8,128)} %shard_map.46.rows_ref), custom_call_target="tpu_custom_call" | custom-call | tf_op jit(solution)/shard_map/pallas_call | solution.py:366

commit v6 on v5

--- a/solution.py
+++ b/solution.py
@@ -124,10 +124,16 @@
     for n in range(4):
         value = back[n * 128 : (n + 1) * 128]
         turned_back.append(value * turn_real - swap(value) * turn_imag)
-    both = times_left(big_ref[1], jnp.concatenate(turned_back, axis=1))
+    return turned_back
+
+
+def finish(blocks, big_ref, roll):
+    lane = lax.broadcasted_iota(jnp.int32, (128, LANES), 1)
+    sign = jnp.where(lane < 64, -1.0, 1.0).astype(jnp.float32)
+    both = times_left(big_ref[1], jnp.concatenate(blocks, axis=1))
     return [
-        both[:128, n * 128 : (n + 1) * 128] + sign * swap(both[128:, n * 128 : (n + 1) * 128])
-        for n in range(4)
+        both[:128, n * 128 : (n + 1) * 128] + sign * roll(both[128:, n * 128 : (n + 1) * 128], 64, 1)
+        for n in range(len(blocks))
     ]
 
 
@@ -256,9 +262,10 @@
     loads[2].wait()
     loads[3].wait()
     first_device = line + plane == 0
-    outcome = correlate(blocks, first_device, big_ref, small_ref, turn_ref, pltpu.roll)
-    for n in range(4):
-        result[n % 2, (n // 2) * 128 : (n // 2) * 128 + 128, :] = outcome[n]
+    turned = correlate(blocks, first_device, big_ref, small_ref, turn_ref, pltpu.roll)
+    at_zero = core == 0
+    given_away = [jnp.where(at_zero, turned[2 * h + 1], turned[2 * h]) for h in range(2)]
+    kept = [jnp.where(at_zero, turned[2 * h], turned[2 * h + 1]) for h in range(2)]
 
     place = z * 32 + plane
     place_mirror = (256 - place) % 256
@@ -271,7 +278,7 @@
 
     swaps = [
         pltpu.make_async_remote_copy(
-            src_ref=result.at[other, half(h)],
+            src_ref=result.at[half(h)],
             dst_ref=paired.at[slots[h], half(h)],
             send_sem=send_core.at[h],
             recv_sem=recv_core.at[h],
@@ -280,15 +287,13 @@
         )
         for h in range(2)
     ]
-    keeps = [
-        pltpu.make_async_copy(
-            result.at[core, half(h)], paired.at[slots[h], half(h)], local.at[2 + h]
-        )
-        for h in range(2)
-    ]
-    for copy in swaps + keeps:
+    for h, value in enumerate(finish(given_away, big_ref, pltpu.roll)):
+        result[half(h)] = value
+    for copy in swaps:
         copy.start()
-    for copy in swaps + keeps:
+    for h, value in enumerate(finish(kept, big_ref, pltpu.roll)):
+        paired[slots[h], half(h)] = value
+    for copy in swaps:
         copy.wait()
 
     for far_x in (2, 1, 3, 0):
@@ -319,7 +324,7 @@
     own = pltpu.make_async_copy(
         paired.at[:, plane_row(y_hi, sheet, z)],
         arrived.at[:, jnp.where(y_hi == 0, place, place_mirror)],
-        local.at[4],
+        local.at[2],
     )
     own.start()
     own.wait()
@@ -355,11 +360,11 @@
             pltpu.VMEM((LINE, PLANE, LANES), jnp.float32),
             pltpu.VMEM((LINE, PLANE, LANES), jnp.float32),
             pltpu.VMEM((4, 8, LINE, LANES), jnp.float32),
-            pltpu.VMEM((2, 256, LANES), jnp.float32),
+            pltpu.VMEM((256, LANES), jnp.float32),
             pltpu.VMEM((2, 256, LANES), jnp.float32),
             pltpu.VMEM((2, 256, LANES), jnp.float32),
             dma((4, LINE)), dma((4, LINE)), dma((PLANE,)), dma((PLANE,)),
-            dma((2,)), dma((2,)), dma((1,)), dma((1,)), dma((5,)), dma((4,)),
+            dma((2,)), dma((2,)), dma((1,)), dma((1,)), dma((3,)), dma((4,)),
         ],
         compiler_params=pltpu.CompilerParams(collective_id=0, has_side_effects=True),
     )(scan_pair, big, small, turns)

time: 49.4 us -> 49.4 us (level)
  no operation moved by 1% of the time
where the time goes in v6:
time: 49.4 us; the launch traced here: 49.3 us
  Pallas kernels  49.3 us (100%)
    pallas_call x1, Pallas kernels, on_device(): pl.pallas_call(kernel, out_shape=jax.ShapeDtypeStruct((ROWS, LANES), jnp....  47.5 us
    pallas_call x1, Pallas kernels, on_device(): pl.pallas_call(turn_kernel, out_shape=jax.ShapeDtypeStruct(scan_pair.shap...  1.79 us

profile of v6, /device:TPU:1, one launch (start us, length us, event | category | flops | bytes accessed | tf_op | source)
XLA Modules:
  0.0 49.3 jit_solution(4275215131247847381)
XLA Ops:
  0.0 47.5 %shard_map.46.rows_ref = f32[512,128]{1,0:T(8,128)} custom-call(f32[2,4,16,512]{3,2,1,0:T(8,128)} %scan_hbm.1, bf16[2,512,256]{2,1,0:T(8,128)(2,1)} %constant.6.clone.big_hbm, bf16[3,256,256]{2,1,0:T(8,128)(2,1)} %constant.7.clone.small_hbm, f32[3,128,128]{2,1,0:T(8,128)} %constant.8.clone.turn_hbm), custom_call_target="tpu_custom_call" | custom-call | tf_op jit(solution)/shard_map/pallas_call | solution.py:350
  47.5 1.8 %shard_map.47 = f32[2,4,16,512]{3,2,1,0:T(8,128)} custom-call(f32[512,128]{1,0:T(8,128)} %shard_map.46.rows_ref), custom_call_target="tpu_custom_call" | custom-call | tf_op jit(solution)/shard_map/pallas_call | solution.py:371
